TPU v7x, 32 devices: a whole 2x2x4 slice. The times are simulated.
32 devices in a mesh: seq: 16 (over z, y, x), ch: 2 (over core).
Axes of the slice: x: 2, y: 2, z: 4, core: 2. Of those that a mesh axis runs over, the one named last changes fastest.
Arguments:
- signal: float32 [4096, 256], P('seq', 'ch'), may hold values from -6 to 6
- decay_rate: float32 [256, 64], P('ch'), may hold values from 0.00024414062 to 0.05
- frequency: float32 [256, 64], P('ch'), may hold values from 0.00024414062 to 0.0625
- coeff_real: float32 [256, 64], P('ch'), may hold values from -0.5 to 0.5
- coeff_imag: float32 [256, 64], P('ch'), may hold values from -0.5 to 0.5
- skip_weight: float32 [256], P('ch'), may hold values from 0.3 to 3
- norm_gain: float32 [256], P('ch'), may hold values from 0.1 to 1.9
Outputs:
- normed: float32 [4096, 256], P('seq', 'ch')
All inputs are finite; a program needn't handle non-finite values.
Results may differ from a plain program's by a relative error of at most 0.00021.
Values sent between devices are 32-bit elements; how exact they have to be, the bound alone decides.
A program may use at most 64 MiB of HBM per device.

v0:
```python
import functools
import math

import jax
import jax.numpy as jnp
from jax import lax
from jax.experimental import pallas as pl
from jax.experimental.pallas import tpu as pltpu
from jax.sharding import PartitionSpec as P

MESH = pl.DeviceIdType.MESH
CHUNK = 128
NT = (((1,), (1,)), ((), ()))
NN = (((1,), (0,)), ((), ()))


def split(value):
    high = value.astype(jnp.bfloat16)
    low = (value - high.astype(jnp.float32)).astype(jnp.bfloat16)
    return high, low


def product(value, high_w, low_w, dims):
    rows = value.shape[0]
    high, low = split(value)
    both = lax.dot_general(
        jnp.concatenate([high, low], axis=0), high_w, dims, preferred_element_type=jnp.float32
    )
    rest = lax.dot_general(high, low_w, dims, preferred_element_type=jnp.float32)
    return both[:rows] + (both[rows:] + rest)


def kernel_body(
    shards,
    halves_of_ch,
    sig_hbm,
    decay_hbm,
    freq_hbm,
    real_hbm,
    imag_hbm,
    skip_ref,
    gain_ref,
    out_ref,
    x_ref,
    params,
    send_a,
    recv_a,
    send_b,
    recv_b,
    skipped,
    in_high,
    in_low,
    out_high,
    out_low,
    near,
    ends_real,
    ends_imag,
    carried,
    mine,
    theirs,
    load_sems,
    send_sems,
    recv_sems,
    own_sems,
    pair_sems,
):
    me = lax.axis_index("seq")
    my_ch = lax.axis_index("ch")
    rows, chans = x_ref.shape
    per_dev = chans // shards
    modes = decay_hbm.shape[1]
    parts = rows // CHUNK
    total = shards * parts

    barrier = pltpu.get_barrier_semaphore()
    for hop in range(1, shards):
        pl.semaphore_signal(
            barrier,
            inc=1,
            device_id={"seq": lax.rem(me + hop, shards), "ch": my_ch},
            device_id_type=MESH,
        )
    for hop in range(1, halves_of_ch):
        pl.semaphore_signal(
            barrier,
            inc=1,
            device_id={"seq": me, "ch": lax.rem(my_ch + hop, halves_of_ch)},
            device_id_type=MESH,
        )

    loads = [pltpu.make_async_copy(sig_hbm, x_ref, load_sems.at[0])]
    for i, ref in enumerate((decay_hbm, freq_hbm, real_hbm, imag_hbm)):
        loads.append(pltpu.make_async_copy(ref, params.at[i], load_sems.at[i + 1]))
    for copy in loads:
        copy.start()
    loads[0].wait()
    turned = x_ref[...].T
    for i in range(shards):
        for part in range(parts):
            send_a[i, part] = turned[
                i * per_dev : (i + 1) * per_dev, part * CHUNK : (part + 1) * CHUNK
            ]

    pl.semaphore_wait(barrier, shards - 1 + halves_of_ch - 1)

    def exchange(source, landing, phase):
        own = pltpu.make_async_copy(source.at[me], landing.at[me], own_sems.at[phase])
        copies = []
        for hop in range(shards - 1, 0, -1):
            target = lax.rem(me + hop, shards)
            copies.append(
                pltpu.make_async_remote_copy(
                    src_ref=source.at[target],
                    dst_ref=landing.at[me],
                    send_sem=send_sems.at[phase, hop],
                    recv_sem=recv_sems.at[phase, hop],
                    device_id={"seq": target, "ch": my_ch},
                    device_id_type=MESH,
                )
            )
        for copy in copies:
            copy.start()
        own.start()
        return own, copies

    own_a, copies_a = exchange(send_a, recv_a, 0)

    skipped[...] = (x_ref[...] * skip_ref[...]).T
    for copy in loads[1:]:
        copy.wait()
    first = me * per_dev
    doubled = []
    for i in range(4):
        row = params[i, pl.ds(first, per_dev), :]
        doubled.append(jnp.concatenate([row, row], axis=1))
    decay, freq, real, imag = doubled
    amplitude = 2.0 * jnp.sqrt(decay)
    real, imag = amplitude * real, amplitude * imag
    lanes = 2 * modes

    def is_imag(count):
        return lax.broadcasted_iota(jnp.int32, (count, lanes), 1) >= modes

    upper = is_imag(per_dev)
    step_real = jnp.exp(-decay) * jnp.cos(freq)
    step_imag = jnp.exp(-decay) * jnp.sin(freq)
    lead_real = real * step_real - imag * step_imag
    lead_imag = real * step_imag + imag * step_real
    lead_real = jnp.where(upper, -lead_real, lead_real)
    weights = jnp.where(upper, -imag, real)
    far_mag = jnp.exp(-decay * CHUNK)
    far_real = far_mag * jnp.cos(freq * CHUNK)
    far_imag = far_mag * jnp.sin(freq * CHUNK)
    far_imag = jnp.where(upper, -far_imag, far_imag)

    groups = CHUNK // 8
    ahead = lax.broadcasted_iota(jnp.int32, (8, lanes), 0).astype(jnp.float32)
    starts = 8.0 * lax.broadcasted_iota(jnp.int32, (groups, lanes), 0).astype(jnp.float32)
    row_id = lax.broadcasted_iota(jnp.int32, (CHUNK, CHUNK), 0)
    col_id = lax.broadcasted_iota(jnp.int32, (CHUNK, CHUNK), 1)
    causal = col_id >= row_id
    quarter = jnp.where(is_imag(8), 0.5 * math.pi, 0.0)

    for c in range(per_dev):
        d_row, f_row = decay[c : c + 1], freq[c : c + 1]
        inner = jnp.exp(-d_row * ahead) * jnp.cos(f_row * ahead - quarter)
        back = 7.0 - ahead
        inner_back = jnp.exp(-d_row * back) * jnp.cos(f_row * back - quarter)
        inner_turned = pltpu.roll(inner, modes, 1)
        inner_back_turned = pltpu.roll(inner_back, modes, 1)
        outer_mag = jnp.exp(-d_row * starts)
        outer_real = outer_mag * jnp.cos(f_row * starts)
        outer_imag = outer_mag * jnp.sin(f_row * starts)
        outer_imag = jnp.where(is_imag(groups), outer_imag, -outer_imag)
        forward, backward = [], []
        for g in range(groups):
            turn_r, turn_i = outer_real[g : g + 1], outer_imag[g : g + 1]
            forward.append(turn_r * inner + turn_i * inner_turned)
            back_r = outer_real[groups - 1 - g : groups - g]
            back_i = outer_imag[groups - 1 - g : groups - g]
            backward.append(back_r * inner_back + back_i * inner_back_turned)
        high, low = split(jnp.concatenate(forward, axis=0))
        out_high[c] = high
        out_low[c] = low
        taps = product(
            jnp.broadcast_to(weights[c : c + 1], (16, lanes)), high, low, NT
        )[0:1]
        spread = pltpu.roll(
            jnp.broadcast_to(taps, (CHUNK, CHUNK)), 0, 1, stride=1, stride_axis=0
        )
        high, low = split(jnp.where(causal, spread, 0.0))
        in_high[c, :, 0:CHUNK] = high
        in_low[c, :, 0:CHUNK] = low
        high, low = split(jnp.concatenate(backward, axis=0))
        in_high[c, :, CHUNK:] = high
        in_low[c, :, CHUNK:] = low

    own_a.wait()
    for copy in copies_a:
        copy.wait_recv()

    strided = per_dev % 8 == 0

    def take(c):
        if strided:
            flat = recv_a.reshape(total * per_dev, CHUNK)
            return flat[pl.ds(c, total, stride=per_dev), :]
        return recv_a[:, :, c, :].reshape(total, CHUNK)

    def put(c, value):
        if strided:
            flat = send_b.reshape(total * per_dev, CHUNK)
            flat[pl.ds(c, total, stride=per_dev), :] = value
        else:
            send_b[:, :, c, :] = value.reshape(shards, parts, CHUNK)

    for c in range(per_dev):
        both = product(take(c), in_high[c], in_low[c], NN)
        near[c] = both[:, :CHUNK]
        ends = both[:, CHUNK:]
        ends_real[pl.ds(c * total, total), :] = ends
        ends_imag[pl.ds(c * total, total), :] = pltpu.roll(ends, modes, 1)

    state_r = jnp.zeros((per_dev, lanes), jnp.float32)
    state_i = jnp.zeros((per_dev, lanes), jnp.float32)

    def advance(shard, state):
        state_r, state_i = state
        for part in range(parts):
            at = pl.ds(shard * parts + part, per_dev, stride=total)
            carried[at, :] = lead_real * state_r - lead_imag * state_i
            next_r = far_real * state_r - far_imag * state_i + ends_real[at, :]
            state_i = far_real * state_i + far_imag * state_r + ends_imag[at, :]
            state_r = next_r
        return state_r, state_i

    if shards <= 16:
        for shard in range(shards):
            state_r, state_i = advance(shard, (state_r, state_i))
    else:
        lax.fori_loop(0, shards, advance, (state_r, state_i))

    for c in range(per_dev):
        state = carried[pl.ds(c * total, total), :]
        value = near[c] + product(state, out_high[c], out_low[c], NT)
        put(c, value)

    own_b, copies_b = exchange(send_b, recv_b, 1)
    own_b.wait()
    for copy in copies_b:
        copy.wait_recv()

    for i in range(shards):
        at = pl.ds(i * per_dev, per_dev)
        for part in range(parts):
            cols = pl.ds(part * CHUNK, CHUNK)
            skipped[at, cols] = recv_b[i, part] + skipped[at, cols]
    summed = skipped[...]
    mine[0:1, :] = jnp.sum(summed, axis=0, keepdims=True)
    mine[1:2, :] = jnp.sum(summed * summed, axis=0, keepdims=True)
    pairs = []
    for hop in range(1, halves_of_ch):
        pairs.append(
            pltpu.make_async_remote_copy(
                src_ref=mine,
                dst_ref=theirs.at[hop - 1],
                send_sem=pair_sems.at[0, hop],
                recv_sem=pair_sems.at[1, hop],
                device_id={"seq": me, "ch": lax.rem(my_ch + hop, halves_of_ch)},
                device_id_type=MESH,
            )
        )
    for copy in pairs:
        copy.start()
    for copy in copies_a + copies_b:
        copy.wait_send()
    for copy in pairs:
        copy.wait()
    sums = mine[...]
    for hop in range(1, halves_of_ch):
        sums = sums + theirs[hop - 1]
    means = sums / (chans * halves_of_ch)
    token_mean = means[0:1]
    token_var = means[1:2] - token_mean * token_mean
    scaled = (summed - token_mean) * lax.rsqrt(token_var + 1e-05)
    out_ref[...] = scaled.T * gain_ref[...]


def on_device(signal, decay_rate, frequency, coeff_real, coeff_imag, skip_weight, norm_gain):
    rows, chans = signal.shape
    shards = lax.axis_size("seq")
    halves_of_ch = lax.axis_size("ch")
    modes = decay_rate.shape[1]
    per_dev = chans // shards
    total = rows // CHUNK * shards
    lanes = 2 * modes
    f32, bf16 = jnp.float32, jnp.bfloat16
    anywhere = pl.BlockSpec(memory_space=pl.ANY)
    vmem = pl.BlockSpec(memory_space=pltpu.VMEM)
    return pl.pallas_call(
        functools.partial(kernel_body, shards, halves_of_ch),
        out_shape=jax.ShapeDtypeStruct((rows, chans), f32),
        in_specs=[anywhere] * 5 + [vmem] * 2,
        out_specs=vmem,
        scratch_shapes=[
            pltpu.VMEM((rows, chans), f32),
            pltpu.VMEM((4, chans, modes), f32),
            pltpu.VMEM((shards, rows // CHUNK, per_dev, CHUNK), f32),
            pltpu.VMEM((shards, rows // CHUNK, per_dev, CHUNK), f32),
            pltpu.VMEM((shards, rows // CHUNK, per_dev, CHUNK), f32),
            pltpu.VMEM((shards, rows // CHUNK, per_dev, CHUNK), f32),
            pltpu.VMEM((chans, rows), f32),
            pltpu.VMEM((per_dev, CHUNK, CHUNK + lanes), bf16),
            pltpu.VMEM((per_dev, CHUNK, CHUNK + lanes), bf16),
            pltpu.VMEM((per_dev, CHUNK, lanes), bf16),
            pltpu.VMEM((per_dev, CHUNK, lanes), bf16),
            pltpu.VMEM((per_dev, total, CHUNK), f32),
            pltpu.VMEM((per_dev * total, lanes), f32),
            pltpu.VMEM((per_dev * total, lanes), f32),
            pltpu.VMEM((per_dev * total, lanes), f32),
            pltpu.VMEM((2, rows), f32),
            pltpu.VMEM((max(halves_of_ch - 1, 1), 2, rows), f32),
            pltpu.SemaphoreType.DMA((5,)),
            pltpu.SemaphoreType.DMA((2, shards)),
            pltpu.SemaphoreType.DMA((2, shards)),
            pltpu.SemaphoreType.DMA((2,)),
            pltpu.SemaphoreType.DMA((2, halves_of_ch)),
        ],
        compiler_params=pltpu.CompilerParams(collective_id=0, has_side_effects=True),
        name="modal_conv",
    )(
        signal,
        decay_rate,
        frequency,
        coeff_real,
        coeff_imag,
        skip_weight.reshape(1, chans),
        norm_gain.reshape(1, chans),
    )


def solution(mesh):
    placed = (
        P("seq", "ch"),
        P("ch", None),
        P("ch", None),
        P("ch", None),
        P("ch", None),
        P("ch"),
        P("ch"),
    )
    return jax.shard_map(
        on_device, mesh=mesh, in_specs=placed, out_specs=P("seq", "ch"), check_vma=False
    )
```

profile of v0, /device:TPU:0, one launch (start us, length us, event | category | flops | bytes accessed | tf_op | source)
XLA Modules:
  0.0 26.1 jit_solution(64109370724168451)
XLA Ops:
  0.0 0.0 copy-start
  0.0 1.5 %copy.8.decay_hbm = f32[128,64]{1,0:T(8,128)} copy(f32[128,64]{0,1:T(8,128)} %param.8) | data formatting | bytes 65536 | tf_op args[1]
  1.5 0.0 copy-done
  1.5 0.0 copy-start.1
  1.5 0.7 %copy.9.freq_hbm = f32[128,64]{1,0:T(8,128)} copy(f32[128,64]{0,1:T(8,128)S(1)} %copy-done) | data formatting | bytes 65536 | tf_op args[2]
  2.2 0.0 copy-done.1
  2.3 0.0 copy-start.2
  2.3 0.7 %copy.10.real_hbm = f32[128,64]{1,0:T(8,128)} copy(f32[128,64]{0,1:T(8,128)S(1)} %copy-done.1) | data formatting | bytes 65536 | tf_op args[3]
  3.0 0.0 copy-done.2
  3.0 0.7 %copy.11.imag_hbm = f32[128,64]{1,0:T(8,128)} copy(f32[128,64]{0,1:T(8,128)S(1)} %copy-done.2) | data formatting | bytes 65536 | tf_op args[4]
  3.7 20.8 %modal_conv.1 = f32[256,128]{1,0:T(8,128)} custom-call(f32[256,128]{1,0:T(8,128)} %sig_hbm.1, f32[128,64]{1,0:T(8,128)} %copy.8.decay_hbm, f32[128,64]{1,0:T(8,128)} %copy.9.freq_hbm, f32[128,64]{1,0:T(8,128)} %copy.10.real_hbm, f32[128,64]{1,0:T(8,128)} %copy.11.imag_hbm, f32[1,128]{1,0:T(1,128)} %bitcast.2, f32[1,128]{1,0:T(1,128)} %bitcast.3), custom_call_target="tpu_custom_call" | custom-call | tf_op jit(solution)/shard_map/modal_conv/pallas_call | solution.py:300
  24.5 1.6 %copy.13 = f32[256,128]{1,0:T(8,128)} copy(f32[256,128]{1,0:T(8,128)} %modal_conv.1) | data formatting | bytes 262144
Async XLA Ops:
  0.0 1.5 %copy-start = (f32[128,64]{0,1:T(8,128)S(1)}, f32[128,64]{0,1:T(8,128)}, u32[]{:S(2)}) copy-start(f32[128,64]{0,1:T(8,128)} %param.9) | copy-start | bytes 98308
  1.5 0.8 %copy-start.1 = (f32[128,64]{0,1:T(8,128)S(1)}, f32[128,64]{0,1:T(8,128)}, u32[]{:S(2)}) copy-start(f32[128,64]{0,1:T(8,128)} %param.10) | copy-start | bytes 98308
  2.3 0.8 %copy-start.2 = (f32[128,64]{0,1:T(8,128)S(1)}, f32[128,64]{0,1:T(8,128)}, u32[]{:S(2)}) copy-start(f32[128,64]{0,1:T(8,128)} %param.11) | copy-start | bytes 98308
where the time goes:
time: 26.5 us; the launch traced here: 26.1 us
  Pallas kernels  20.8 us (78%)
  local copies, waits for them, and re-layouts  5.31 us (20%)
    pallas_call x1, Pallas kernels, on_device(): pl.pallas_call(functools.partial(kernel_body, shards, halves_of_ch), out_...  20.8 us
    unnamed x11, local copies, waits for them, and re-layouts  5.31 us

commit v1 on v0

--- a/solution.py
+++ b/solution.py
@@ -39,7 +39,6 @@
     real_hbm,
     imag_hbm,
     skip_ref,
-    gain_ref,
     out_ref,
     x_ref,
     params,
@@ -47,7 +46,8 @@
     recv_a,
     send_b,
     recv_b,
-    skipped,
+    sums_to,
+    sums_from,
     in_high,
     in_low,
     out_high,
@@ -56,8 +56,7 @@
     ends_real,
     ends_imag,
     carried,
-    mine,
-    theirs,
+    owned,
     load_sems,
     send_sems,
     recv_sems,
@@ -68,7 +67,7 @@
     my_ch = lax.axis_index("ch")
     rows, chans = x_ref.shape
     per_dev = chans // shards
-    modes = decay_hbm.shape[1]
+    modes = decay_hbm.shape[0]
     parts = rows // CHUNK
     total = shards * parts
 
@@ -80,13 +79,17 @@
             device_id={"seq": lax.rem(me + hop, shards), "ch": my_ch},
             device_id_type=MESH,
         )
-    for hop in range(1, halves_of_ch):
-        pl.semaphore_signal(
-            barrier,
-            inc=1,
-            device_id={"seq": me, "ch": lax.rem(my_ch + hop, halves_of_ch)},
-            device_id_type=MESH,
-        )
+    for side in range(1, halves_of_ch):
+        for hop in range(shards):
+            pl.semaphore_signal(
+                barrier,
+                inc=1,
+                device_id={
+                    "seq": lax.rem(me + hop, shards),
+                    "ch": lax.rem(my_ch + side, halves_of_ch),
+                },
+                device_id_type=MESH,
+            )
 
     loads = [pltpu.make_async_copy(sig_hbm, x_ref, load_sems.at[0])]
     for i, ref in enumerate((decay_hbm, freq_hbm, real_hbm, imag_hbm)):
@@ -101,7 +104,7 @@
                 i * per_dev : (i + 1) * per_dev, part * CHUNK : (part + 1) * CHUNK
             ]
 
-    pl.semaphore_wait(barrier, shards - 1 + halves_of_ch - 1)
+    pl.semaphore_wait(barrier, shards * halves_of_ch - 1)
 
     def exchange(source, landing, phase):
         own = pltpu.make_async_copy(source.at[me], landing.at[me], own_sems.at[phase])
@@ -125,15 +128,13 @@
 
     own_a, copies_a = exchange(send_a, recv_a, 0)
 
-    skipped[...] = (x_ref[...] * skip_ref[...]).T
     for copy in loads[1:]:
         copy.wait()
-    first = me * per_dev
-    doubled = []
     for i in range(4):
-        row = params[i, pl.ds(first, per_dev), :]
-        doubled.append(jnp.concatenate([row, row], axis=1))
-    decay, freq, real, imag = doubled
+        owned[i] = jnp.concatenate([params[i], params[i]], axis=0).T
+    owned[4] = jnp.broadcast_to(skip_ref[...], (2 * modes, chans)).T
+    mine = pl.ds(me * per_dev, per_dev)
+    decay, freq, real, imag, skip = [owned[i, mine, :] for i in range(5)]
     amplitude = 2.0 * jnp.sqrt(decay)
     real, imag = amplitude * real, amplitude * imag
     lanes = 2 * modes
@@ -215,8 +216,9 @@
             send_b[:, :, c, :] = value.reshape(shards, parts, CHUNK)
 
     for c in range(per_dev):
-        both = product(take(c), in_high[c], in_low[c], NN)
-        near[c] = both[:, :CHUNK]
+        signal = take(c)
+        both = product(signal, in_high[c], in_low[c], NN)
+        near[c] = both[:, :CHUNK] + skip[c : c + 1] * signal
         ends = both[:, CHUNK:]
         ends_real[pl.ds(c * total, total), :] = ends
         ends_imag[pl.ds(c * total, total), :] = pltpu.roll(ends, modes, 1)
@@ -240,50 +242,60 @@
     else:
         lax.fori_loop(0, shards, advance, (state_r, state_i))
 
+    total_sum = jnp.zeros((total, CHUNK), jnp.float32)
+    total_square = jnp.zeros((total, CHUNK), jnp.float32)
     for c in range(per_dev):
         state = carried[pl.ds(c * total, total), :]
         value = near[c] + product(state, out_high[c], out_low[c], NT)
+        total_sum = total_sum + value
+        total_square = total_square + value * value
         put(c, value)
 
+    for shard in range(shards):
+        rows_of = slice(shard * parts, (shard + 1) * parts)
+        sums_to[shard, 0:parts] = total_sum[rows_of]
+        sums_to[shard, parts : 2 * parts] = total_square[rows_of]
+
     own_b, copies_b = exchange(send_b, recv_b, 1)
+    sums_copies = []
+    for side in range(1, halves_of_ch):
+        for hop in range(shards - 1, -1, -1):
+            target = lax.rem(me + hop, shards)
+            sums_copies.append(
+                pltpu.make_async_remote_copy(
+                    src_ref=sums_to.at[target],
+                    dst_ref=sums_from.at[side - 1, me],
+                    send_sem=pair_sems.at[0, side - 1, hop],
+                    recv_sem=pair_sems.at[1, side - 1, hop],
+                    device_id={"seq": target, "ch": lax.rem(my_ch + side, halves_of_ch)},
+                    device_id_type=MESH,
+                )
+            )
+    for copy in sums_copies:
+        copy.start()
     own_b.wait()
     for copy in copies_b:
         copy.wait_recv()
-
-    for i in range(shards):
-        at = pl.ds(i * per_dev, per_dev)
-        for part in range(parts):
-            cols = pl.ds(part * CHUNK, CHUNK)
-            skipped[at, cols] = recv_b[i, part] + skipped[at, cols]
-    summed = skipped[...]
-    mine[0:1, :] = jnp.sum(summed, axis=0, keepdims=True)
-    mine[1:2, :] = jnp.sum(summed * summed, axis=0, keepdims=True)
-    pairs = []
-    for hop in range(1, halves_of_ch):
-        pairs.append(
-            pltpu.make_async_remote_copy(
-                src_ref=mine,
-                dst_ref=theirs.at[hop - 1],
-                send_sem=pair_sems.at[0, hop],
-                recv_sem=pair_sems.at[1, hop],
-                device_id={"seq": me, "ch": lax.rem(my_ch + hop, halves_of_ch)},
-                device_id_type=MESH,
-            )
-        )
-    for copy in pairs:
-        copy.start()
-    for copy in copies_a + copies_b:
+    own_sums, own_squares, blocks = [], [], []
+    for part in range(parts):
+        block = jnp.concatenate([recv_b[i, part] for i in range(shards)], axis=0)
+        blocks.append(block)
+        own_sums.append(jnp.sum(block, axis=0, keepdims=True))
+        own_squares.append(jnp.sum(block * block, axis=0, keepdims=True))
+    sums = jnp.concatenate(own_sums + own_squares, axis=0)
+    for copy in sums_copies:
+        copy.wait_recv()
+    for side in range(halves_of_ch - 1):
+        for shard in range(shards):
+            sums = sums + sums_from[side, shard]
+    means = sums / (chans * halves_of_ch)
+    for part in range(parts):
+        token_mean = means[part : part + 1]
+        token_var = means[parts + part : parts + part + 1] - token_mean * token_mean
+        scaled = (blocks[part] - token_mean) * lax.rsqrt(token_var + 1e-05)
+        out_ref[part * CHUNK : (part + 1) * CHUNK, :] = scaled.T
+    for copy in copies_a + copies_b + sums_copies:
         copy.wait_send()
-    for copy in pairs:
-        copy.wait()
-    sums = mine[...]
-    for hop in range(1, halves_of_ch):
-        sums = sums + theirs[hop - 1]
-    means = sums / (chans * halves_of_ch)
-    token_mean = means[0:1]
-    token_var = means[1:2] - token_mean * token_mean
-    scaled = (summed - token_mean) * lax.rsqrt(token_var + 1e-05)
-    out_ref[...] = scaled.T * gain_ref[...]
 
 
 def on_device(signal, decay_rate, frequency, coeff_real, coeff_imag, skip_weight, norm_gain):
@@ -292,24 +304,26 @@
     halves_of_ch = lax.axis_size("ch")
     modes = decay_rate.shape[1]
     per_dev = chans // shards
-    total = rows // CHUNK * shards
+    parts = rows // CHUNK
+    total = parts * shards
     lanes = 2 * modes
     f32, bf16 = jnp.float32, jnp.bfloat16
     anywhere = pl.BlockSpec(memory_space=pl.ANY)
     vmem = pl.BlockSpec(memory_space=pltpu.VMEM)
-    return pl.pallas_call(
+    normed = pl.pallas_call(
         functools.partial(kernel_body, shards, halves_of_ch),
         out_shape=jax.ShapeDtypeStruct((rows, chans), f32),
-        in_specs=[anywhere] * 5 + [vmem] * 2,
+        in_specs=[anywhere] * 5 + [vmem],
         out_specs=vmem,
         scratch_shapes=[
             pltpu.VMEM((rows, chans), f32),
-            pltpu.VMEM((4, chans, modes), f32),
+            pltpu.VMEM((4, modes, chans), f32),
             pltpu.VMEM((shards, rows // CHUNK, per_dev, CHUNK), f32),
             pltpu.VMEM((shards, rows // CHUNK, per_dev, CHUNK), f32),
             pltpu.VMEM((shards, rows // CHUNK, per_dev, CHUNK), f32),
             pltpu.VMEM((shards, rows // CHUNK, per_dev, CHUNK), f32),
-            pltpu.VMEM((chans, rows), f32),
+            pltpu.VMEM((shards, 2 * parts, CHUNK), f32),
+            pltpu.VMEM((max(halves_of_ch - 1, 1), shards, 2 * parts, CHUNK), f32),
             pltpu.VMEM((per_dev, CHUNK, CHUNK + lanes), bf16),
             pltpu.VMEM((per_dev, CHUNK, CHUNK + lanes), bf16),
             pltpu.VMEM((per_dev, CHUNK, lanes), bf16),
@@ -318,25 +332,24 @@
             pltpu.VMEM((per_dev * total, lanes), f32),
             pltpu.VMEM((per_dev * total, lanes), f32),
             pltpu.VMEM((per_dev * total, lanes), f32),
-            pltpu.VMEM((2, rows), f32),
-            pltpu.VMEM((max(halves_of_ch - 1, 1), 2, rows), f32),
+            pltpu.VMEM((5, chans, lanes), f32),
             pltpu.SemaphoreType.DMA((5,)),
             pltpu.SemaphoreType.DMA((2, shards)),
             pltpu.SemaphoreType.DMA((2, shards)),
             pltpu.SemaphoreType.DMA((2,)),
-            pltpu.SemaphoreType.DMA((2, halves_of_ch)),
+            pltpu.SemaphoreType.DMA((2, max(halves_of_ch - 1, 1), shards)),
         ],
         compiler_params=pltpu.CompilerParams(collective_id=0, has_side_effects=True),
         name="modal_conv",
     )(
         signal,
-        decay_rate,
-        frequency,
-        coeff_real,
-        coeff_imag,
+        decay_rate.T,
+        frequency.T,
+        coeff_real.T,
+        coeff_imag.T,
         skip_weight.reshape(1, chans),
-        norm_gain.reshape(1, chans),
     )
+    return normed * norm_gain[None, :]
 
 
 def solution(mesh):

time: 26.5 us -> 22.5 us (0.85)
  local copies, waits for them, and re-layouts: 5.31 us -> 0.01 us
  other arithmetic: 0 us -> 1.57 us
    unnamed x11 -> x2, local copies, waits for them, and re-layouts: 5.31 us -> 0.01 us
    mul x0 -> x1, other arithmetic: none -> 1.57 us  [on_device(): return normed * norm_gain[None, :]]
where the time goes in v1:
time: 22.5 us; the launch traced here: 22.4 us
  Pallas kernels  20.8 us (92%)
  other arithmetic  1.57 us (7%)
    pallas_call x1, Pallas kernels, on_device(): pl.pallas_call(functools.partial(kernel_body, shards, halves_of_ch), out_...  20.8 us
    mul x1, other arithmetic, on_device(): return normed * norm_gain[None, :]  1.57 us

profile of v1, /device:TPU:0, one launch (start us, length us, event | category | flops | bytes accessed | tf_op | source)
XLA Modules:
  0.0 22.4 jit_solution(4827518390605853617)
XLA Ops:
  0.0 0.0 copy-start
  0.0 20.8 %modal_conv.1 = f32[256,128]{1,0:T(8,128)} custom-call(f32[256,128]{1,0:T(8,128)} %sig_hbm.1, f32[64,128]{1,0:T(8,128)} %bitcast.5, f32[64,128]{1,0:T(8,128)} %bitcast.6, f32[64,128]{1,0:T(8,128)} %bitcast.7, f32[64,128]{1,0:T(8,128)} %bitcast.8, f32[1,128]{1,0:T(1,128)} %bitcast.9), custom_call_target="tpu_custom_call" | custom-call | tf_op jit(solution)/shard_map/modal_conv/pallas_call | solution.py:313
  20.8 0.0 copy-done
  20.8 1.6 %broadcast_multiply_fusion = f32[256,128]{1,0:T(8,128)} fusion(f32[256,128]{1,0:T(8,128)} %modal_conv.1, f32[128]{0:T(128)S(1)} %copy-done), kind=kLoop, calls=%fused_computation | loop fusion | flops 32768 | bytes 262656 | tf_op jit(solution)/shard_map/mul | solution.py:352
Async XLA Ops:
  0.0 20.8 %copy-start = (f32[128]{0:T(128)S(1)}, f32[128]{0:T(128)}, u32[]{:S(2)}) copy-start(f32[128]{0:T(128)} %param.13) | copy-start | bytes 1540

commit v2 on v1

--- a/solution.py
+++ b/solution.py
@@ -115,8 +115,8 @@
                 pltpu.make_async_remote_copy(
                     src_ref=source.at[target],
                     dst_ref=landing.at[me],
-                    send_sem=send_sems.at[phase, hop],
-                    recv_sem=recv_sems.at[phase, hop],
+                    send_sem=send_sems.at[phase],
+                    recv_sem=recv_sems.at[phase],
                     device_id={"seq": target, "ch": my_ch},
                     device_id_type=MESH,
                 )
@@ -124,9 +124,12 @@
         for copy in copies:
             copy.start()
         own.start()
-        return own, copies
-
-    own_a, copies_a = exchange(send_a, recv_a, 0)
+        others = landing.at[pl.ds(0, shards - 1)]
+        arrived = pltpu.make_async_copy(others, others, recv_sems.at[phase])
+        departed = pltpu.make_async_copy(others, others, send_sems.at[phase])
+        return own, arrived, departed
+
+    own_a, arrived_a, departed_a = exchange(send_a, recv_a, 0)
 
     for copy in loads[1:]:
         copy.wait()
@@ -197,8 +200,7 @@
         in_low[c, :, CHUNK:] = low
 
     own_a.wait()
-    for copy in copies_a:
-        copy.wait_recv()
+    arrived_a.wait()
 
     strided = per_dev % 8 == 0
 
@@ -256,7 +258,7 @@
         sums_to[shard, 0:parts] = total_sum[rows_of]
         sums_to[shard, parts : 2 * parts] = total_square[rows_of]
 
-    own_b, copies_b = exchange(send_b, recv_b, 1)
+    own_b, arrived_b, departed_b = exchange(send_b, recv_b, 1)
     sums_copies = []
     for side in range(1, halves_of_ch):
         for hop in range(shards - 1, -1, -1):
@@ -265,8 +267,8 @@
                 pltpu.make_async_remote_copy(
                     src_ref=sums_to.at[target],
                     dst_ref=sums_from.at[side - 1, me],
-                    send_sem=pair_sems.at[0, side - 1, hop],
-                    recv_sem=pair_sems.at[1, side - 1, hop],
+                    send_sem=pair_sems.at[0],
+                    recv_sem=pair_sems.at[1],
                     device_id={"seq": target, "ch": lax.rem(my_ch + side, halves_of_ch)},
                     device_id_type=MESH,
                 )
@@ -274,8 +276,7 @@
     for copy in sums_copies:
         copy.start()
     own_b.wait()
-    for copy in copies_b:
-        copy.wait_recv()
+    arrived_b.wait()
     own_sums, own_squares, blocks = [], [], []
     for part in range(parts):
         block = jnp.concatenate([recv_b[i, part] for i in range(shards)], axis=0)
@@ -283,8 +284,8 @@
         own_sums.append(jnp.sum(block, axis=0, keepdims=True))
         own_squares.append(jnp.sum(block * block, axis=0, keepdims=True))
     sums = jnp.concatenate(own_sums + own_squares, axis=0)
-    for copy in sums_copies:
-        copy.wait_recv()
+    if sums_copies:
+        pltpu.make_async_copy(sums_from, sums_from, pair_sems.at[1]).wait()
     for side in range(halves_of_ch - 1):
         for shard in range(shards):
             sums = sums + sums_from[side, shard]
@@ -294,8 +295,10 @@
         token_var = means[parts + part : parts + part + 1] - token_mean * token_mean
         scaled = (blocks[part] - token_mean) * lax.rsqrt(token_var + 1e-05)
         out_ref[part * CHUNK : (part + 1) * CHUNK, :] = scaled.T
-    for copy in copies_a + copies_b + sums_copies:
-        copy.wait_send()
+    departed_a.wait()
+    departed_b.wait()
+    if sums_copies:
+        pltpu.make_async_copy(sums_from, sums_from, pair_sems.at[0]).wait()
 
 
 def on_device(signal, decay_rate, frequency, coeff_real, coeff_imag, skip_weight, norm_gain):
@@ -312,7 +315,7 @@
     vmem = pl.BlockSpec(memory_space=pltpu.VMEM)
     normed = pl.pallas_call(
         functools.partial(kernel_body, shards, halves_of_ch),
-        out_shape=jax.ShapeDtypeStruct((rows, chans), f32),
+        out_shape=pltpu.VMEM((rows, chans), f32),
         in_specs=[anywhere] * 5 + [vmem],
         out_specs=vmem,
         scratch_shapes=[
@@ -334,10 +337,10 @@
             pltpu.VMEM((per_dev * total, lanes), f32),
             pltpu.VMEM((5, chans, lanes), f32),
             pltpu.SemaphoreType.DMA((5,)),
-            pltpu.SemaphoreType.DMA((2, shards)),
-            pltpu.SemaphoreType.DMA((2, shards)),
             pltpu.SemaphoreType.DMA((2,)),
-            pltpu.SemaphoreType.DMA((2, max(halves_of_ch - 1, 1), shards)),
+            pltpu.SemaphoreType.DMA((2,)),
+            pltpu.SemaphoreType.DMA((2,)),
+            pltpu.SemaphoreType.DMA((2,)),
         ],
         compiler_params=pltpu.CompilerParams(collective_id=0, has_side_effects=True),
         name="modal_conv",

time: 22.5 us -> 20 us (0.89)
  Pallas kernels: 20.8 us -> 19.2 us
  other arithmetic: 1.57 us -> 0.67 us
    pallas_call x1, Pallas kernels: 20.8 us -> 19.2 us  [on_device(): pl.pallas_call(functools.partial(kernel_body, shards, halves_of_ch), out_...]
    mul x1, other arithmetic: 1.57 us -> 0.67 us  [on_device(): return normed * norm_gain[None, :]]
where the time goes in v2:
time: 20 us; the launch traced here: 19.9 us
  Pallas kernels  19.2 us (96%)
  other arithmetic  0.67 us (3%)
    pallas_call x1, Pallas kernels, on_device(): pl.pallas_call(functools.partial(kernel_body, shards, halves_of_ch), out_...  19.2 us
    mul x1, other arithmetic, on_device(): return normed * norm_gain[None, :]  0.67 us

profile of v2, /device:TPU:0, one launch (start us, length us, event | category | flops | bytes accessed | tf_op | source)
XLA Modules:
  0.0 19.9 jit_solution(17876862051379356825)
XLA Ops:
  0.0 0.0 copy-start
  0.0 19.2 %modal_conv.1 = f32[256,128]{1,0:T(8,128)S(1)} custom-call(f32[256,128]{1,0:T(8,128)} %sig_hbm.1, f32[64,128]{1,0:T(8,128)} %bitcast.5, f32[64,128]{1,0:T(8,128)} %bitcast.6, f32[64,128]{1,0:T(8,128)} %bitcast.7, f32[64,128]{1,0:T(8,128)} %bitcast.8, f32[1,128]{1,0:T(1,128)} %bitcast.9), custom_call_target="tpu_custom_call" | custom-call | tf_op jit(solution)/shard_map/modal_conv/pallas_call | solution.py:316
  19.2 0.0 copy-done
  19.2 0.7 %broadcast_multiply_fusion = f32[256,128]{1,0:T(8,128)} fusion(f32[256,128]{1,0:T(8,128)S(1)} %modal_conv.1, f32[128]{0:T(128)S(1)} %copy-done), kind=kLoop, calls=%fused_computation | loop fusion | flops 32768 | bytes 262656 | tf_op jit(solution)/shard_map/mul | solution.py:355
Async XLA Ops:
  0.0 19.2 %copy-start = (f32[128]{0:T(128)S(1)}, f32[128]{0:T(128)}, u32[]{:S(2)}) copy-start(f32[128]{0:T(128)} %param.13) | copy-start | bytes 1540

commit v3 on v2

v3 whole, which is shorter than its diff:
```python
import functools
import math

import jax
import jax.numpy as jnp
from jax import lax
from jax.experimental import pallas as pl
from jax.experimental.pallas import tpu as pltpu
from jax.sharding import PartitionSpec as P

MESH = pl.DeviceIdType.MESH
CHUNK = 128
NT = (((1,), (1,)), ((), ()))
NN = (((1,), (0,)), ((), ()))


def split(value):
    high = value.astype(jnp.bfloat16)
    low = (value - high.astype(jnp.float32)).astype(jnp.bfloat16)
    return high, low


def product(value, high_w, low_w, dims):
    rows = value.shape[0]
    high = value.astype(jnp.bfloat16).astype(jnp.float32)
    both = jnp.concatenate([high, value - high], axis=0).astype(jnp.bfloat16)
    out = lax.dot_general(both, high_w, dims, preferred_element_type=jnp.float32)
    out = out + lax.dot_general(both, low_w, dims, preferred_element_type=jnp.float32)
    return out[:rows] + out[rows:]


def kernel_body(
    inner,
    outer,
    halves_of_ch,
    sig_hbm,
    decay_hbm,
    freq_hbm,
    real_hbm,
    imag_hbm,
    skip_ref,
    out_ref,
    x_ref,
    params,
    send_a,
    recv_a,
    send_b,
    recv_b,
    sums_to,
    sums_from,
    end_high,
    end_low,
    near_high,
    near_low,
    out_high,
    out_low,
    near,
    ends_real,
    ends_imag,
    carried,
    owned,
    plane_to,
    plane_from,
    load_sems,
    send_sems,
    recv_sems,
    own_sems,
    pair_sems,
    plane_sems,
):
    me = lax.axis_index("seq")
    my_ch = lax.axis_index("ch")
    rows, chans = x_ref.shape
    my_outer, my_inner = me // inner, lax.rem(me, inner)
    base = my_outer * inner
    per_dev = chans // inner
    modes = decay_hbm.shape[0]
    parts = rows // CHUNK
    total = inner * parts

    barrier = pltpu.get_barrier_semaphore()
    peers = []
    for hop in range(1, outer):
        peers.append((lax.rem(my_outer + hop, outer) * inner + my_inner, my_ch))
    for side in range(halves_of_ch):
        for hop in range(1 if side == 0 else 0, inner):
            peers.append(
                (base + lax.rem(my_inner + hop, inner), lax.rem(my_ch + side, halves_of_ch))
            )
    for seq, ch in peers:
        pl.semaphore_signal(
            barrier, inc=1, device_id={"seq": seq, "ch": ch}, device_id_type=MESH
        )

    loads = [pltpu.make_async_copy(sig_hbm, x_ref, load_sems.at[0])]
    for i, ref in enumerate((decay_hbm, freq_hbm, real_hbm, imag_hbm)):
        loads.append(pltpu.make_async_copy(ref, params.at[i], load_sems.at[i + 1]))
    for copy in loads:
        copy.start()
    loads[0].wait()
    turned = x_ref[...].T
    for i in range(inner):
        for part in range(parts):
            send_a[i, part] = turned[
                i * per_dev : (i + 1) * per_dev, part * CHUNK : (part + 1) * CHUNK
            ]

    def exchange(source, landing, phase):
        own = pltpu.make_async_copy(
            source.at[my_inner], landing.at[my_inner], own_sems.at[phase]
        )
        copies = []
        for hop in range(inner - 1, 0, -1):
            target = lax.rem(my_inner + hop, inner)
            copies.append(
                pltpu.make_async_remote_copy(
                    src_ref=source.at[target],
                    dst_ref=landing.at[my_inner],
                    send_sem=send_sems.at[phase],
                    recv_sem=recv_sems.at[phase],
                    device_id={"seq": base + target, "ch": my_ch},
                    device_id_type=MESH,
                )
            )
        for copy in copies:
            copy.start()
        own.start()
        others = landing.at[pl.ds(0, inner - 1)]
        arrived = pltpu.make_async_copy(others, others, recv_sems.at[phase])
        departed = pltpu.make_async_copy(others, others, send_sems.at[phase])
        return own, arrived, departed

    for copy in loads[1:]:
        copy.wait()
    for i in range(4):
        owned[i] = jnp.concatenate([params[i], params[i]], axis=0).T
    owned[4] = jnp.broadcast_to(skip_ref[...], (2 * modes, chans)).T
    mine = pl.ds(my_inner * per_dev, per_dev)
    decay, freq, real, imag, skip = [owned[i, mine, :] for i in range(5)]
    amplitude = 2.0 * jnp.sqrt(decay)
    real, imag = amplitude * real, amplitude * imag
    lanes = 2 * modes

    def is_imag(count):
        return lax.broadcasted_iota(jnp.int32, (count, lanes), 1) >= modes

    upper = is_imag(per_dev)
    step_real = jnp.exp(-decay) * jnp.cos(freq)
    step_imag = jnp.exp(-decay) * jnp.sin(freq)
    lead_real = real * step_real - imag * step_imag
    lead_imag = real * step_imag + imag * step_real
    lead_real = jnp.where(upper, -lead_real, lead_real)
    weights = jnp.where(upper, -imag, real)
    far_mag = jnp.exp(-decay * CHUNK)
    far_real = far_mag * jnp.cos(freq * CHUNK)
    far_imag = far_mag * jnp.sin(freq * CHUNK)
    far_imag = jnp.where(upper, -far_imag, far_imag)
    plane_mag = jnp.exp(-decay * (CHUNK * total))
    plane_real = plane_mag * jnp.cos(freq * (CHUNK * total))
    plane_imag = plane_mag * jnp.sin(freq * (CHUNK * total))
    plane_imag = jnp.where(upper, -plane_imag, plane_imag)

    groups = CHUNK // 8
    ahead = lax.broadcasted_iota(jnp.int32, (8, lanes), 0).astype(jnp.float32)
    starts = 8.0 * lax.broadcasted_iota(jnp.int32, (groups, lanes), 0).astype(jnp.float32)
    row_id = lax.broadcasted_iota(jnp.int32, (CHUNK, CHUNK), 0)
    col_id = lax.broadcasted_iota(jnp.int32, (CHUNK, CHUNK), 1)
    causal = col_id >= row_id
    quarter = jnp.where(is_imag(8), 0.5 * math.pi, 0.0)

    def build(c):
        d_row, f_row = decay[c : c + 1], freq[c : c + 1]
        inner = jnp.exp(-d_row * ahead) * jnp.cos(f_row * ahead - quarter)
        back = 7.0 - ahead
        inner_back = jnp.exp(-d_row * back) * jnp.cos(f_row * back - quarter)
        inner_turned = pltpu.roll(inner, modes, 1)
        inner_back_turned = pltpu.roll(inner_back, modes, 1)
        outer_mag = jnp.exp(-d_row * starts)
        outer_real = outer_mag * jnp.cos(f_row * starts)
        outer_imag = outer_mag * jnp.sin(f_row * starts)
        outer_imag = jnp.where(is_imag(groups), outer_imag, -outer_imag)
        forward, backward = [], []
        for g in range(groups):
            turn_r, turn_i = outer_real[g : g + 1], outer_imag[g : g + 1]
            forward.append(turn_r * inner + turn_i * inner_turned)
            back_r = outer_real[groups - 1 - g : groups - g]
            back_i = outer_imag[groups - 1 - g : groups - g]
            backward.append(back_r * inner_back + back_i * inner_back_turned)
        high, low = split(jnp.concatenate(forward, axis=0))
        out_high[c] = high
        out_low[c] = low
        taps = product(
            jnp.broadcast_to(weights[c : c + 1], (16, lanes)), high, low, NT
        )[0:1]
        spread = pltpu.roll(
            jnp.broadcast_to(taps, (CHUNK, CHUNK)), 0, 1, stride=1, stride_axis=0
        )
        high, low = split(jnp.where(causal, spread, 0.0))
        near_high[c] = high
        near_low[c] = low
        high, low = split(jnp.concatenate(backward, axis=0))
        end_high[c] = high
        end_low[c] = low

    for c in range(per_dev // 2):
        build(c)
    pl.semaphore_wait(barrier, len(peers))
    own_a, arrived_a, departed_a = exchange(send_a, recv_a, 0)
    for c in range(per_dev // 2, per_dev):
        build(c)

    own_a.wait()
    arrived_a.wait()

    strided = per_dev % 8 == 0

    def take(c):
        if strided:
            flat = recv_a.reshape(total * per_dev, CHUNK)
            return flat[pl.ds(c, total, stride=per_dev), :]
        return recv_a[:, :, c, :].reshape(total, CHUNK)

    def put(c, value):
        if strided:
            flat = send_b.reshape(total * per_dev, CHUNK)
            flat[pl.ds(c, total, stride=per_dev), :] = value
        else:
            send_b[:, :, c, :] = value.reshape(inner, parts, CHUNK)

    for c in range(per_dev):
        ends = product(take(c), end_high[c], end_low[c], NN)
        ends_real[pl.ds(c * total, total), :] = ends
        ends_imag[pl.ds(c * total, total), :] = pltpu.roll(ends, modes, 1)

    def advance(state_r, state_i, chunk, keep):
        at = pl.ds(chunk, per_dev, stride=total)
        if keep:
            carried[at, :] = lead_real * state_r - lead_imag * state_i
        next_r = far_real * state_r - far_imag * state_i + ends_real[at, :]
        next_i = far_real * state_i + far_imag * state_r + ends_imag[at, :]
        return next_r, next_i

    zero = jnp.zeros((per_dev, lanes), jnp.float32)
    state_r, state_i = zero, zero
    for chunk in range(total):
        state_r, state_i = advance(state_r, state_i, chunk, False)
    plane_to[...] = state_r
    plane_from[my_outer] = state_r
    plane_copies = []
    for hop in range(outer - 1, 0, -1):
        target = lax.rem(my_outer + hop, outer)
        plane_copies.append(
            pltpu.make_async_remote_copy(
                src_ref=plane_to,
                dst_ref=plane_from.at[my_outer],
                send_sem=plane_sems.at[0],
                recv_sem=plane_sems.at[1],
                device_id={"seq": target * inner + my_inner, "ch": my_ch},
                device_id_type=MESH,
            )
        )
    for copy in plane_copies:
        copy.start()

    for c in range(per_dev):
        signal = take(c)
        near[c] = product(signal, near_high[c], near_low[c], NN) + skip[c : c + 1] * signal

    others = plane_from.at[pl.ds(0, outer - 1)]
    pltpu.make_async_copy(others, others, plane_sems.at[1]).wait()
    state_r, state_i = zero, zero
    for plane in range(outer - 1):
        before = plane < my_outer
        left_r = plane_from[plane]
        left_i = pltpu.roll(left_r, modes, 1)
        next_r = plane_real * state_r - plane_imag * state_i + left_r
        next_i = plane_real * state_i + plane_imag * state_r + left_i
        state_r = jnp.where(before, next_r, state_r)
        state_i = jnp.where(before, next_i, state_i)
    for chunk in range(total):
        state_r, state_i = advance(state_r, state_i, chunk, True)

    total_sum = jnp.zeros((total, CHUNK), jnp.float32)
    total_square = jnp.zeros((total, CHUNK), jnp.float32)
    for c in range(per_dev):
        state = carried[pl.ds(c * total, total), :]
        value = near[c] + product(state, out_high[c], out_low[c], NT)
        total_sum = total_sum + value
        total_square = total_square + value * value
        put(c, value)

    for shard in range(inner):
        rows_of = slice(shard * parts, (shard + 1) * parts)
        sums_to[shard, 0:parts] = total_sum[rows_of]
        sums_to[shard, parts : 2 * parts] = total_square[rows_of]

    own_b, arrived_b, departed_b = exchange(send_b, recv_b, 1)
    sums_copies = []
    for side in range(1, halves_of_ch):
        for hop in range(inner - 1, -1, -1):
            target = lax.rem(my_inner + hop, inner)
            sums_copies.append(
                pltpu.make_async_remote_copy(
                    src_ref=sums_to.at[target],
                    dst_ref=sums_from.at[side - 1, my_inner],
                    send_sem=pair_sems.at[0],
                    recv_sem=pair_sems.at[1],
                    device_id={
                        "seq": base + target,
                        "ch": lax.rem(my_ch + side, halves_of_ch),
                    },
                    device_id_type=MESH,
                )
            )
    for copy in sums_copies:
        copy.start()
    own_b.wait()
    arrived_b.wait()
    own_sums, own_squares, blocks = [], [], []
    for part in range(parts):
        block = jnp.concatenate([recv_b[i, part] for i in range(inner)], axis=0)
        blocks.append(block)
        own_sums.append(jnp.sum(block, axis=0, keepdims=True))
        own_squares.append(jnp.sum(block * block, axis=0, keepdims=True))
    sums = jnp.concatenate(own_sums + own_squares, axis=0)
    if sums_copies:
        pltpu.make_async_copy(sums_from, sums_from, pair_sems.at[1]).wait()
    for side in range(halves_of_ch - 1):
        for shard in range(inner):
            sums = sums + sums_from[side, shard]
    means = sums / (chans * halves_of_ch)
    for part in range(parts):
        token_mean = means[part : part + 1]
        token_var = means[parts + part : parts + part + 1] - token_mean * token_mean
        scaled = (blocks[part] - token_mean) * lax.rsqrt(token_var + 1e-05)
        out_ref[part * CHUNK : (part + 1) * CHUNK, :] = scaled.T
    departed_a.wait()
    departed_b.wait()
    pltpu.make_async_copy(others, others, plane_sems.at[0]).wait()
    if sums_copies:
        pltpu.make_async_copy(sums_from, sums_from, pair_sems.at[0]).wait()


def on_device(signal, decay_rate, frequency, coeff_real, coeff_imag, skip_weight, norm_gain):
    rows, chans = signal.shape
    shards = lax.axis_size("seq")
    halves_of_ch = lax.axis_size("ch")
    modes = decay_rate.shape[1]
    inner = 1
    while (2 * inner) ** 2 <= shards:
        inner *= 2
    outer = shards // inner
    per_dev = chans // inner
    parts = rows // CHUNK
    total = parts * inner
    lanes = 2 * modes
    f32, bf16 = jnp.float32, jnp.bfloat16
    anywhere = pl.BlockSpec(memory_space=pl.ANY)
    vmem = pl.BlockSpec(memory_space=pltpu.VMEM)
    normed = pl.pallas_call(
        functools.partial(kernel_body, inner, outer, halves_of_ch),
        out_shape=pltpu.VMEM((rows, chans), f32),
        in_specs=[anywhere] * 5 + [vmem],
        out_specs=vmem,
        scratch_shapes=[
            pltpu.VMEM((rows, chans), f32),
            pltpu.VMEM((4, modes, chans), f32),
            pltpu.VMEM((inner, parts, per_dev, CHUNK), f32),
            pltpu.VMEM((inner, parts, per_dev, CHUNK), f32),
            pltpu.VMEM((inner, parts, per_dev, CHUNK), f32),
            pltpu.VMEM((inner, parts, per_dev, CHUNK), f32),
            pltpu.VMEM((inner, 2 * parts, CHUNK), f32),
            pltpu.VMEM((max(halves_of_ch - 1, 1), inner, 2 * parts, CHUNK), f32),
            pltpu.VMEM((per_dev, CHUNK, lanes), bf16),
            pltpu.VMEM((per_dev, CHUNK, lanes), bf16),
            pltpu.VMEM((per_dev, CHUNK, CHUNK), bf16),
            pltpu.VMEM((per_dev, CHUNK, CHUNK), bf16),
            pltpu.VMEM((per_dev, CHUNK, lanes), bf16),
            pltpu.VMEM((per_dev, CHUNK, lanes), bf16),
            pltpu.VMEM((per_dev, total, CHUNK), f32),
            pltpu.VMEM((per_dev * total, lanes), f32),
            pltpu.VMEM((per_dev * total, lanes), f32),
            pltpu.VMEM((per_dev * total, lanes), f32),
            pltpu.VMEM((5, chans, lanes), f32),
            pltpu.VMEM((per_dev, lanes), f32),
            pltpu.VMEM((outer, per_dev, lanes), f32),
            pltpu.SemaphoreType.DMA((5,)),
            pltpu.SemaphoreType.DMA((2,)),
            pltpu.SemaphoreType.DMA((2,)),
            pltpu.SemaphoreType.DMA((2,)),
            pltpu.SemaphoreType.DMA((2,)),
            pltpu.SemaphoreType.DMA((2,)),
        ],
        compiler_params=pltpu.CompilerParams(collective_id=0, has_side_effects=True),
        name="modal_conv",
    )(
        signal,
        decay_rate.T,
        frequency.T,
        coeff_real.T,
        coeff_imag.T,
        skip_weight.reshape(1, chans),
    )
    return normed * norm_gain[None, :]


def solution(mesh):
    placed = (
        P("seq", "ch"),
        P("ch", None),
        P("ch", None),
        P("ch", None),
        P("ch", None),
        P("ch"),
        P("ch"),
    )
    return jax.shard_map(
        on_device, mesh=mesh, in_specs=placed, out_specs=P("seq", "ch"), check_vma=False
    )
```

time: 20 us -> 21.6 us (1.080)
  Pallas kernels: 19.2 us -> 20.7 us
    pallas_call x1, Pallas kernels: 19.2 us -> 20.7 us  [on_device(): pl.pallas_call(functools.partial(kernel_body, inner, outer, halves_of_ch)...]
where the time goes in v3:
time: 21.6 us; the launch traced here: 21.4 us
  Pallas kernels  20.7 us (96%)
  other arithmetic  0.67 us (3%)
    pallas_call x1, Pallas kernels, on_device(): pl.pallas_call(functools.partial(kernel_body, inner, outer, halves_of_ch)...  20.7 us
    mul x1, other arithmetic, on_device(): return normed * norm_gain[None, :]  0.67 us

profile of v3, /device:TPU:0, one launch (start us, length us, event | category | flops | bytes accessed | tf_op | source)
XLA Modules:
  0.0 21.4 jit_solution(8238558227925960340)
XLA Ops:
  0.0 0.0 copy-start
  0.0 20.7 %modal_conv.1 = f32[256,128]{1,0:T(8,128)S(1)} custom-call(f32[256,128]{1,0:T(8,128)} %sig_hbm.1, f32[64,128]{1,0:T(8,128)} %bitcast.5, f32[64,128]{1,0:T(8,128)} %bitcast.6, f32[64,128]{1,0:T(8,128)} %bitcast.7, f32[64,128]{1,0:T(8,128)} %bitcast.8, f32[1,128]{1,0:T(1,128)} %bitcast.9), custom_call_target="tpu_custom_call" | custom-call | tf_op jit(solution)/shard_map/modal_conv/pallas_call | solution.py:360
  20.7 0.0 copy-done
  20.7 0.7 %broadcast_multiply_fusion = f32[256,128]{1,0:T(8,128)} fusion(f32[256,128]{1,0:T(8,128)S(1)} %modal_conv.1, f32[128]{0:T(128)S(1)} %copy-done), kind=kLoop, calls=%fused_computation | loop fusion | flops 32768 | bytes 262656 | tf_op jit(solution)/shard_map/mul | solution.py:404
Async XLA Ops:
  0.0 20.7 %copy-start = (f32[128]{0:T(128)S(1)}, f32[128]{0:T(128)}, u32[]{:S(2)}) copy-start(f32[128]{0:T(128)} %param.13) | copy-start | bytes 1540

commit v4 on v3

--- a/solution.py
+++ b/solution.py
@@ -20,13 +20,13 @@
     return high, low
 
 
-def product(value, high_w, low_w, dims):
+def product(value, weights, dims):
     rows = value.shape[0]
     high = value.astype(jnp.bfloat16).astype(jnp.float32)
     both = jnp.concatenate([high, value - high], axis=0).astype(jnp.bfloat16)
-    out = lax.dot_general(both, high_w, dims, preferred_element_type=jnp.float32)
-    out = out + lax.dot_general(both, low_w, dims, preferred_element_type=jnp.float32)
-    return out[:rows] + out[rows:]
+    out = lax.dot_general(both, weights, dims, preferred_element_type=jnp.float32)
+    width = out.shape[1] // 2
+    return out[:rows, :width] + (out[rows:, :width] + out[:rows, width:])
 
 
 def kernel_body(
@@ -48,12 +48,9 @@
     recv_b,
     sums_to,
     sums_from,
-    end_high,
-    end_low,
-    near_high,
-    near_low,
-    out_high,
-    out_low,
+    end_w,
+    near_w,
+    out_w,
     near,
     ends_real,
     ends_imag,
@@ -130,6 +127,8 @@
         departed = pltpu.make_async_copy(others, others, send_sems.at[phase])
         return own, arrived, departed
 
+    pl.semaphore_wait(barrier, len(peers))
+    own_a, arrived_a, departed_a = exchange(send_a, recv_a, 0)
     for copy in loads[1:]:
         copy.wait()
     for i in range(4):
@@ -187,26 +186,20 @@
             back_i = outer_imag[groups - 1 - g : groups - g]
             backward.append(back_r * inner_back + back_i * inner_back_turned)
         high, low = split(jnp.concatenate(forward, axis=0))
-        out_high[c] = high
-        out_low[c] = low
+        joined = jnp.concatenate([high, low], axis=0)
+        out_w[c] = joined
         taps = product(
-            jnp.broadcast_to(weights[c : c + 1], (16, lanes)), high, low, NT
+            jnp.broadcast_to(weights[c : c + 1], (8, lanes)), joined, NT
         )[0:1]
         spread = pltpu.roll(
             jnp.broadcast_to(taps, (CHUNK, CHUNK)), 0, 1, stride=1, stride_axis=0
         )
         high, low = split(jnp.where(causal, spread, 0.0))
-        near_high[c] = high
-        near_low[c] = low
+        near_w[c] = jnp.concatenate([high, low], axis=1)
         high, low = split(jnp.concatenate(backward, axis=0))
-        end_high[c] = high
-        end_low[c] = low
-
-    for c in range(per_dev // 2):
-        build(c)
-    pl.semaphore_wait(barrier, len(peers))
-    own_a, arrived_a, departed_a = exchange(send_a, recv_a, 0)
-    for c in range(per_dev // 2, per_dev):
+        end_w[c] = jnp.concatenate([high, low], axis=1)
+
+    for c in range(per_dev):
         build(c)
 
     own_a.wait()
@@ -228,7 +221,7 @@
             send_b[:, :, c, :] = value.reshape(inner, parts, CHUNK)
 
     for c in range(per_dev):
-        ends = product(take(c), end_high[c], end_low[c], NN)
+        ends = product(take(c), end_w[c], NN)
         ends_real[pl.ds(c * total, total), :] = ends
         ends_imag[pl.ds(c * total, total), :] = pltpu.roll(ends, modes, 1)
 
@@ -264,7 +257,7 @@
 
     for c in range(per_dev):
         signal = take(c)
-        near[c] = product(signal, near_high[c], near_low[c], NN) + skip[c : c + 1] * signal
+        near[c] = product(signal, near_w[c], NN) + skip[c : c + 1] * signal
 
     others = plane_from.at[pl.ds(0, outer - 1)]
     pltpu.make_async_copy(others, others, plane_sems.at[1]).wait()
@@ -284,7 +277,7 @@
     total_square = jnp.zeros((total, CHUNK), jnp.float32)
     for c in range(per_dev):
         state = carried[pl.ds(c * total, total), :]
-        value = near[c] + product(state, out_high[c], out_low[c], NT)
+        value = near[c] + product(state, out_w[c], NT)
         total_sum = total_sum + value
         total_square = total_square + value * value
         put(c, value)
@@ -371,12 +364,9 @@
             pltpu.VMEM((inner, parts, per_dev, CHUNK), f32),
             pltpu.VMEM((inner, 2 * parts, CHUNK), f32),
             pltpu.VMEM((max(halves_of_ch - 1, 1), inner, 2 * parts, CHUNK), f32),
-            pltpu.VMEM((per_dev, CHUNK, lanes), bf16),
-            pltpu.VMEM((per_dev, CHUNK, lanes), bf16),
-            pltpu.VMEM((per_dev, CHUNK, CHUNK), bf16),
-            pltpu.VMEM((per_dev, CHUNK, CHUNK), bf16),
-            pltpu.VMEM((per_dev, CHUNK, lanes), bf16),
-            pltpu.VMEM((per_dev, CHUNK, lanes), bf16),
+            pltpu.VMEM((per_dev, CHUNK, 2 * lanes), bf16),
+            pltpu.VMEM((per_dev, CHUNK, 2 * CHUNK), bf16),
+            pltpu.VMEM((per_dev, 2 * CHUNK, lanes), bf16),
             pltpu.VMEM((per_dev, total, CHUNK), f32),
             pltpu.VMEM((per_dev * total, lanes), f32),
             pltpu.VMEM((per_dev * total, lanes), f32),

time: 21.6 us -> 19.8 us (0.917)
  Pallas kernels: 20.7 us -> 19 us
    pallas_call x1, Pallas kernels: 20.7 us -> 19 us  [on_device(): pl.pallas_call(functools.partial(kernel_body, inner, outer, halves_of_ch)...]
where the time goes in v4:
time: 19.8 us; the launch traced here: 19.6 us
  Pallas kernels  19 us (96%)
  other arithmetic  0.67 us (3%)
    pallas_call x1, Pallas kernels, on_device(): pl.pallas_call(functools.partial(kernel_body, inner, outer, halves_of_ch)...  19 us
    mul x1, other arithmetic, on_device(): return normed * norm_gain[None, :]  0.67 us

profile of v4, /device:TPU:0, one launch (start us, length us, event | category | flops | bytes accessed | tf_op | source)
XLA Modules:
  0.0 19.6 jit_solution(15477659041527885175)
XLA Ops:
  0.0 0.0 copy-start
  0.0 19.0 %modal_conv.1 = f32[256,128]{1,0:T(8,128)S(1)} custom-call(f32[256,128]{1,0:T(8,128)} %sig_hbm.1, f32[64,128]{1,0:T(8,128)} %bitcast.5, f32[64,128]{1,0:T(8,128)} %bitcast.6, f32[64,128]{1,0:T(8,128)} %bitcast.7, f32[64,128]{1,0:T(8,128)} %bitcast.8, f32[1,128]{1,0:T(1,128)} %bitcast.9), custom_call_target="tpu_custom_call" | custom-call | tf_op jit(solution)/shard_map/modal_conv/pallas_call | solution.py:353
  19.0 0.0 copy-done
  19.0 0.7 %broadcast_multiply_fusion = f32[256,128]{1,0:T(8,128)} fusion(f32[256,128]{1,0:T(8,128)S(1)} %modal_conv.1, f32[128]{0:T(128)S(1)} %copy-done), kind=kLoop, calls=%fused_computation | loop fusion | flops 32768 | bytes 262656 | tf_op jit(solution)/shard_map/mul | solution.py:394
Async XLA Ops:
  0.0 19.0 %copy-start = (f32[128]{0:T(128)S(1)}, f32[128]{0:T(128)}, u32[]{:S(2)}) copy-start(f32[128]{0:T(128)} %param.13) | copy-start | bytes 1540
